TPU v7x, 512 devices: a whole 4x4x16 slice. The times are simulated.
512 devices in a mesh: dom: 16 (over x, y_lo, core), shard: 32 (over y_hi, z).
Axes of the slice: x: 4, y: 4 (y_hi: 2, y_lo: 2; y = y_hi * 2 + y_lo), z: 16, core: 2. Of those that a mesh axis runs over, the one named last changes fastest.
Arguments:
- embeddings: float32 [32768, 400], P(('dom', 'shard')), may hold values from -3 to 3
- row_accum: float32 [32768], P(('dom', 'shard')), may hold values from 0.01 to 1
- relations: bfloat16 [2560, 400], replicated, may hold values from -3 to 3
- relation_accum: float32 [2560], P(('dom', 'shard')), may hold values from 0.01 to 1
- request_rows: int32 [2, 16384, 2, 16], P(None, ('dom', 'shard')), may hold values from 0 to 63
- head_slots: int32 [2, 65536], P(None, ('dom', 'shard')), may hold values from 0 to 511
- tail_slots: int32 [2, 65536], P(None, ('dom', 'shard')), may hold values from 0 to 511
- relation_ids: int32 [2, 65536], P(None, ('dom', 'shard')), may hold values from 0 to 2559
- own_negatives: int32 [2, 262144], P(None, ('dom', 'shard')), may hold values from 0 to 511
- far_negatives: int32 [2, 262144], P(None, ('dom', 'shard')), may hold values from 0 to 511
Outputs:
- new_embeddings: float32 [32768, 400], P(('dom', 'shard'))
- new_accum: float32 [32768], P(('dom', 'shard'))
- relation_step: float32 [2560, 400], P(('dom', 'shard'))
- new_relation_accum: float32 [2560], P(('dom', 'shard'))
Inputs may be any that keep to these rules, and one draw needn't show every extreme that they name: `request_rows`: local row numbers within the owner's 64 rows. `head_slots`: slots of the 512 own-side touched rows. `tail_slots`: slots of the 512 partner-side touched rows. `own_negatives`: slots of the 512 own-side touched rows. `far_negatives`: slots of the 512 partner-side touched rows.
All inputs are finite; a program needn't handle non-finite values.
Results may differ from a plain program's by a relative error of at most 0.0049.
Values may be sent and summed in bfloat16 or wider, within the bound.
A program may use at most 64 MiB of HBM per device.

v0:
```python
import jax
import jax.numpy as jnp
from jax import lax
from jax.sharding import PartitionSpec as P

LEARN_RATE = 0.1
BF = jnp.bfloat16
F32 = jnp.float32


def partner(value, axis, distance):
    mask = 2**distance
    pairs = [(source, source ^ mask) for source in range(lax.axis_size(axis))]
    return lax.ppermute(value, axis, pairs)


def mm(a, b, ca, cb):
    return lax.dot_general(a, b, (((ca,), (cb,)), ((), ())), preferred_element_type=F32)


def one_hot(ids, n):
    return (ids[:, None] == jnp.arange(n, dtype=ids.dtype)[None, :]).astype(BF)


def split_mm(a, b, ca, cb):
    hi = b.astype(BF)
    lo = (b - hi.astype(F32)).astype(BF)
    return mm(a, hi, ca, cb) + mm(a, lo, ca, cb)


def edge_terms(own, far, head_slots, tail_slots, rel_vec, own_neg, far_neg):
    touch = own.shape[0]
    neg = own_neg.shape[0]
    head_hot = one_hot(head_slots, touch)
    tail_hot = one_hot(tail_slots, touch)
    head_vec = mm(head_hot, own, 1, 0)
    tail_vec = mm(tail_hot, far, 1, 0)
    slots = jnp.arange(touch, dtype=own_neg.dtype)
    own_count = jnp.sum((own_neg[:, None] == slots[None, :]).astype(F32), axis=0)
    far_count = jnp.sum((far_neg[:, None] == slots[None, :]).astype(F32), axis=0)
    positive = jnp.sum(head_vec * rel_vec * tail_vec, axis=-1)
    query_tail = (head_vec * rel_vec).astype(BF)
    query_head = (tail_vec * rel_vec).astype(BF)
    score_tail = mm(query_tail, far, 1, 1)
    score_head = mm(query_head, own, 1, 1)
    weight_tail = (jax.nn.sigmoid(score_tail) * (far_count / neg)).astype(BF)
    weight_head = (jax.nn.sigmoid(score_head) * (own_count / neg)).astype(BF)
    back_tail = mm(weight_tail, far, 1, 0)
    back_head = mm(weight_head, own, 1, 0)
    coeff = -jax.nn.sigmoid(-positive)[:, None]
    grad_head = rel_vec * (coeff * tail_vec + back_tail)
    grad_tail = rel_vec * (coeff * head_vec + back_head)
    grad_rel = coeff * head_vec * tail_vec + head_vec * back_tail + tail_vec * back_head
    own_grad = split_mm(head_hot, grad_head, 0, 0) + mm(weight_head, query_head, 0, 0)
    far_grad = split_mm(tail_hot, grad_tail, 0, 0) + mm(weight_tail, query_tail, 0, 0)
    return (own_grad.astype(BF), far_grad.astype(BF), grad_rel)


def body(
    embeddings,
    row_accum,
    relations,
    relation_accum,
    request_rows,
    head_slots,
    tail_slots,
    relation_ids,
    own_negatives,
    far_negatives,
):
    rows, width = embeddings.shape
    shards = lax.axis_size("shard")
    slot_count = request_rows.shape[-1]
    touch = shards * slot_count
    rounds = request_rows.shape[0]
    emb = embeddings
    accum = row_accum
    rel_rows = []
    all_rel = relations[relation_ids.reshape(-1)].astype(F32).reshape(rounds, -1, width)
    for r in range(rounds):
        lowered = emb.astype(BF)
        ids = request_rows[r].reshape(-1)
        hot = one_hot(ids, rows)
        served = mm(hot, lowered, 1, 0).astype(BF).reshape(shards, 2, slot_count, width)
        received = lax.all_to_all(served, "shard", split_axis=0, concat_axis=0, tiled=True)
        own = received[:, 0].reshape(touch, width)
        far = partner(received[:, 1].reshape(touch, width), "dom", r)
        own_grad, far_grad, grad_rel = edge_terms(
            own, far, head_slots[r], tail_slots[r], all_rel[r], own_negatives[r], far_negatives[r]
        )
        rel_rows.append(grad_rel.astype(BF))
        far_back = partner(far_grad, "dom", r)
        outgoing = jnp.stack(
            [
                own_grad.reshape(shards, slot_count, width),
                far_back.reshape(shards, slot_count, width),
            ],
            axis=1,
        )
        returned = lax.all_to_all(outgoing, "shard", split_axis=0, concat_axis=0, tiled=True)
        row_grad = mm(hot, returned.reshape(-1, width), 0, 0)
        accum = accum + jnp.mean(row_grad * row_grad, axis=-1)
        emb = emb - LEARN_RATE * row_grad / jnp.sqrt(accum)[:, None]
    mine = jnp.concatenate(rel_rows, axis=0)
    ids = lax.all_gather(relation_ids.reshape(-1), "dom", tiled=True)
    group_rows = lax.all_gather(mine, "dom", tiled=True)
    per_group = relations.shape[0] // lax.axis_size("dom")
    local = ids - lax.axis_index("dom").astype(ids.dtype) * per_group
    dense = mm(one_hot(local, per_group), group_rows, 0, 0)
    pieces = dense.reshape(shards, per_group // shards, width)
    pieces = lax.all_to_all(pieces, "shard", split_axis=0, concat_axis=0, tiled=True)
    own_share = jnp.sum(pieces, axis=0)
    new_relation_accum = relation_accum + jnp.mean(own_share * own_share, axis=-1)
    relation_step = -LEARN_RATE * own_share / jnp.sqrt(new_relation_accum)[:, None]
    return (emb, accum, relation_step, new_relation_accum)


def solution(mesh):
    both = ("dom", "shard")
    return jax.shard_map(
        body,
        mesh=mesh,
        in_specs=(P(both, None), P(both), P(), P(both), P(None, both, None, None))
        + (P(None, both),) * 5,
        out_specs=(P(both, None), P(both), P(both, None), P(both)),
        check_vma=False,
    )
```

profile of v0, /device:TPU:2, one launch (start us, length us, event | category | flops | bytes accessed | tf_op | source)
XLA Modules:
  0.0 351.7 jit_solution(11925494591055917611)
XLA Ops:
  7.2 0.7 fusion.69
  8.1 1.5 convolution_convert_fusion.1
  9.6 1.3 copy.43
  10.9 18.2 %all-to-all-start = ((bf16[32,2,16,400]{3,2,1,0:T(8,128)(2,1)}), bf16[32,2,16,400]{3,2,1,0:T(8,128)(2,1)}, u32[]{:S(2)}, u32[]{:S(2)}) async-start(bf16[32,2,16,400]{3,2,1,0:T(8,128)(2,1)} %bitcast.3), calls=%async_computation | async-start | bytes 2097152 | tf_op jit(solution)/shard_map/all_to_all | solution.py:85
  29.1 2.9 copy.41
  32.1 1.2 gather_fusion
  33.9 47.7 %all-to-all-done = bf16[32,2,16,400]{3,2,1,0:T(8,128)(2,1)} async-done(((bf16[32,2,16,400]{3,2,1,0:T(8,128)(2,1)}), bf16[32,2,16,400]{3,2,1,0:T(8,128)(2,1)}, u32[]{:S(2)}, u32[]{:S(2)}) %all-to-all-start) | async-done | bytes 819232 | tf_op jit(solution)/shard_map/all_to_all | solution.py:85
  81.5 1.3 fusion.68
  82.8 1.9 collective-permute-start
  84.8 1.8 collective-permute-done
  86.6 0.4 fusion.35
  87.0 0.4 fusion.52
  87.4 0.4 fusion.22
  89.8 2.0 collective-permute-start.1
  93.0 0.4 collective-permute-done.1
  93.8 1.1 copy.46
  94.8 7.9 %all-to-all-start.1 = ((bf16[32,2,16,400]{3,2,1,0:T(8,128)(2,1)}), bf16[32,2,16,400]{3,2,1,0:T(8,128)(2,1)S(1)}, u32[]{:S(2)}, u32[]{:S(2)}) async-start(bf16[32,2,16,400]{3,2,1,0:T(8,128)(2,1)} %copy.46), calls=%async_computation.1 | async-start | bytes 2097152 | tf_op jit(solution)/shard_map/all_to_all | solution.py:100
  103.0 52.4 %all-to-all-done.1 = bf16[32,2,16,400]{3,2,1,0:T(8,128)(2,1)S(1)} async-done(((bf16[32,2,16,400]{3,2,1,0:T(8,128)(2,1)}), bf16[32,2,16,400]{3,2,1,0:T(8,128)(2,1)S(1)}, u32[]{:S(2)}, u32[]{:S(2)}) %all-to-all-start.1) | async-done | bytes 819232 | tf_op jit(solution)/shard_map/all_to_all | solution.py:100
  155.3 0.6 multiply_reduce_fusion.3
  155.9 0.6 convolution_convert_fusion
  156.5 1.3 copy.48
  157.8 8.1 %all-to-all-start.2 = ((bf16[32,2,16,400]{3,2,1,0:T(8,128)(2,1)}), bf16[32,2,16,400]{3,2,1,0:T(8,128)(2,1)S(1)}, u32[]{:S(2)}, u32[]{:S(2)}) async-start(bf16[32,2,16,400]{3,2,1,0:T(8,128)(2,1)} %bitcast.13), calls=%async_computation.2 | async-start | bytes 2097152 | tf_op jit(solution)/shard_map/all_to_all | solution.py:85
  166.3 51.9 %all-to-all-done.2 = bf16[32,2,16,400]{3,2,1,0:T(8,128)(2,1)S(1)} async-done(((bf16[32,2,16,400]{3,2,1,0:T(8,128)(2,1)}), bf16[32,2,16,400]{3,2,1,0:T(8,128)(2,1)S(1)}, u32[]{:S(2)}, u32[]{:S(2)}) %all-to-all-start.2) | async-done | bytes 819232 | tf_op jit(solution)/shard_map/all_to_all | solution.py:85
  218.4 2.6 collective-permute-start.2
  221.0 11.5 %collective-permute-done.2 = bf16[512,400]{1,0:T(8,128)(2,1)S(1)} collective-permute-done((bf16[512,400]{1,0:T(8,128)(2,1)S(1)}, bf16[512,400]{1,0:T(8,128)(2,1)S(1)}, u32[]{:S(2)}, u32[]{:S(2)}) %collective-permute-start.2) | collective-permute-done | bytes 409632 | tf_op jit(solution)/shard_map/ppermute | solution.py:14
  232.4 0.4 fusion.29
  232.8 0.4 fusion.53
  233.2 0.4 fusion.24
  233.9 0.4 fusion.25
  234.6 0.7 pad_maximum_fusion.2
  236.3 2.8 collective-permute-start.3
  240.3 6.8 %collective-permute-done.3 = bf16[512,400]{0,1:T(8,128)(2,1)S(1)} collective-permute-done((bf16[512,400]{0,1:T(8,128)(2,1)S(1)}, bf16[512,400]{0,1:T(8,128)(2,1)S(1)}, u32[]{:S(2)}, u32[]{:S(2)}) %collective-permute-start.3) | collective-permute-done | bytes 409632 | tf_op jit(solution)/shard_map/ppermute | solution.py:14
  247.4 1.1 copy.51
  248.5 11.0 %all-to-all-start.3 = ((bf16[32,2,16,400]{3,2,1,0:T(8,128)(2,1)}), bf16[32,2,16,400]{3,2,1,0:T(8,128)(2,1)S(1)}, u32[]{:S(2)}, u32[]{:S(2)}) async-start(bf16[32,2,16,400]{3,2,1,0:T(8,128)(2,1)} %copy.51), calls=%async_computation.3 | async-start | bytes 2097152 | tf_op jit(solution)/shard_map/all_to_all | solution.py:100
  259.5 16.7 %all-gather = s32[16,1,256]{2,1,0:T(1,128)S(1)} all-gather(s32[1,1,256]{2,1,0:T(1,128)S(1)} %bitcast.82), channel_id=1, replica_groups=mesh['dom'=16,'shard'=32] {'dom'}, dimensions={0}, use_global_device_ids=true | all-gather | bytes 17408 | tf_op jit(solution)/shard_map/all_gather | solution.py:105
  276.2 5.0 %all-gather.3.cloned.1.call-done = bf16[4096,400]{0,1:T(8,128)(2,1)} async-done(((bf16[256,400]{0,1:T(8,128)(2,1)}), bf16[4096,400]{0,1:T(8,128)(2,1)}) %all-gather.3.cloned.1.call-update) | async-done | bytes 3276816 | tf_op jit(solution)/shard_map/all_gather | solution.py:106
  281.2 3.0 fusion
  284.4 1.3 reshape.122
  285.6 25.2 %all-to-all-done.3 = bf16[32,2,16,400]{3,2,1,0:T(8,128)(2,1)S(1)} async-done(((bf16[32,2,16,400]{3,2,1,0:T(8,128)(2,1)}), bf16[32,2,16,400]{3,2,1,0:T(8,128)(2,1)S(1)}, u32[]{:S(2)}, u32[]{:S(2)}) %all-to-all-start.3) | async-done | bytes 819232 | tf_op jit(solution)/shard_map/all_to_all | solution.py:100
  310.9 7.4 %all-to-all-start.4 = ((f32[32,1,2000]{2,1,0:T(1,128)}), f32[32,1,2000]{2,1,0:T(1,128)S(1)}, u32[]{:S(2)}, u32[]{:S(2)}) async-start(f32[32,1,2000]{2,1,0:T(1,128)} %reshape.122), calls=%async_computation.4 | async-start | bytes 524288 | tf_op jit(solution)/shard_map/all_to_all | solution.py:111
  318.3 0.6 multiply_reduce_fusion.2
  318.9 0.5 fusion.66
  319.4 0.8 divide_subtract_fusion
  320.2 21.2 %all-to-all-done.4 = f32[32,1,2000]{2,1,0:T(1,128)S(1)} async-done(((f32[32,1,2000]{2,1,0:T(1,128)}), f32[32,1,2000]{2,1,0:T(1,128)S(1)}, u32[]{:S(2)}, u32[]{:S(2)}) %all-to-all-start.4) | async-done | bytes 256032 | tf_op jit(solution)/shard_map/all_to_all | solution.py:111
  341.3 0.5 broadcast.114
  341.9 1.3 reduce
  343.6 0.5 fusion.65
  344.2 0.7 multiply_divide_fusion
  (70 shorter events, 8.6 us)
Async XLA Ops:
  10.9 70.7 %all-to-all-start = ((bf16[32,2,16,400]{3,2,1,0:T(8,128)(2,1)}), bf16[32,2,16,400]{3,2,1,0:T(8,128)(2,1)}, u32[]{:S(2)}, u32[]{:S(2)}) async-start(bf16[32,2,16,400]{3,2,1,0:T(8,128)(2,1)} %bitcast.3), calls=%async_computation | async-start | bytes 2097152 | tf_op jit(solution)/shard_map/all_to_all | solution.py:85
  29.1 2.9 copy-start.1
  32.0 1.4 copy-start.2
  32.0 1.6 copy-start.3
  32.0 1.8 copy-start.4
  32.1 52.7 %copy-start.5 = (s32[2,128]{1,0:T(2,128)S(1)}, s32[2,128]{1,0:T(2,128)}, u32[]{:S(2)}) copy-start(s32[2,128]{1,0:T(2,128)} %param.15) | copy-start | bytes 3076
  82.8 3.8 %collective-permute-start = (bf16[512,400]{1,0:T(8,128)(2,1)S(1)}, bf16[512,400]{1,0:T(8,128)(2,1)S(1)}, u32[]{:S(2)}, u32[]{:S(2)}) collective-permute-start(bf16[512,400]{1,0:T(8,128)(2,1)S(1)} %bitcast.73), channel_id=1, source_target_pairs={{0,32},{32,0},{64,96},{96,64},{128,160},{160,128},{192,224},{224,1... | collective-permute-start | bytes 1228808 | tf_op jit(solution)/shard_map/ppermute | solution.py:14
  89.8 3.6 %collective-permute-start.1 = (bf16[512,400]{0,1:T(8,128)(2,1)S(1)}, bf16[512,400]{0,1:T(8,128)(2,1)S(1)}, u32[]{:S(2)}, u32[]{:S(2)}) collective-permute-start(bf16[512,400]{0,1:T(8,128)(2,1)S(1)} %fusion.3), channel_id=1, source_target_pairs={{0,32},{32,0},{64,96},{96,64},{128,160},{160,128},{192,224},{224,1... | collective-permute-start | bytes 1228808 | tf_op jit(solution)/shard_map/ppermute | solution.py:14
  93.7 62.1 %copy-start.6 = (f32[64]{0:T(128)S(1)}, f32[64]{0:T(128)}, u32[]{:S(2)}) copy-start(f32[64]{0:T(128)} %param.11) | copy-start | bytes 772
  93.8 62.2 %copy-start = (f32[64,400]{1,0:T(8,128)S(1)}, f32[64,400]{1,0:T(8,128)}, u32[]{:S(2)}) copy-start(f32[64,400]{1,0:T(8,128)} %param.10) | copy-start | bytes 307204
  94.8 60.5 %all-to-all-start.1 = ((bf16[32,2,16,400]{3,2,1,0:T(8,128)(2,1)}), bf16[32,2,16,400]{3,2,1,0:T(8,128)(2,1)S(1)}, u32[]{:S(2)}, u32[]{:S(2)}) async-start(bf16[32,2,16,400]{3,2,1,0:T(8,128)(2,1)} %copy.46), calls=%async_computation.1 | async-start | bytes 2097152 | tf_op jit(solution)/shard_map/all_to_all | solution.py:100
  157.8 60.5 %all-to-all-start.2 = ((bf16[32,2,16,400]{3,2,1,0:T(8,128)(2,1)}), bf16[32,2,16,400]{3,2,1,0:T(8,128)(2,1)S(1)}, u32[]{:S(2)}, u32[]{:S(2)}) async-start(bf16[32,2,16,400]{3,2,1,0:T(8,128)(2,1)} %bitcast.13), calls=%async_computation.2 | async-start | bytes 2097152 | tf_op jit(solution)/shard_map/all_to_all | solution.py:85
  165.9 115.3 %all-gather.3.cloned.1.call-start = ((), (), s32[]{:S(2)}) async-start(), calls=%async_computation.5 | async-start | bytes 3481600 | tf_op jit(solution)/shard_map/all_gather | solution.py:106
  218.4 14.1 %collective-permute-start.2 = (bf16[512,400]{1,0:T(8,128)(2,1)S(1)}, bf16[512,400]{1,0:T(8,128)(2,1)S(1)}, u32[]{:S(2)}, u32[]{:S(2)}) collective-permute-start(bf16[512,400]{1,0:T(8,128)(2,1)S(1)} %bitcast.74), channel_id=1, source_target_pairs={{0,64},{32,96},{64,0},{96,32},{128,192},{160,224},{192,128},{224,1... | collective-permute-start | bytes 1228808 | tf_op jit(solution)/shard_map/ppermute | solution.py:14
  236.3 10.7 %collective-permute-start.3 = (bf16[512,400]{0,1:T(8,128)(2,1)S(1)}, bf16[512,400]{0,1:T(8,128)(2,1)S(1)}, u32[]{:S(2)}, u32[]{:S(2)}) collective-permute-start(bf16[512,400]{0,1:T(8,128)(2,1)S(1)} %fusion.5), channel_id=1, source_target_pairs={{0,64},{32,96},{64,0},{96,32},{128,192},{160,224},{192,128},{224,1... | collective-permute-start | bytes 1228808 | tf_op jit(solution)/shard_map/ppermute | solution.py:14
  248.5 62.3 %all-to-all-start.3 = ((bf16[32,2,16,400]{3,2,1,0:T(8,128)(2,1)}), bf16[32,2,16,400]{3,2,1,0:T(8,128)(2,1)S(1)}, u32[]{:S(2)}, u32[]{:S(2)}) async-start(bf16[32,2,16,400]{3,2,1,0:T(8,128)(2,1)} %copy.51), calls=%async_computation.3 | async-start | bytes 2097152 | tf_op jit(solution)/shard_map/all_to_all | solution.py:100
  284.4 59.3 %copy-start.7 = (f32[5]{0:T(128)S(1)}, f32[5]{0:T(128)}, u32[]{:S(2)}) copy-start(f32[5]{0:T(128)} %param.13) | copy-start | bytes 64
  310.9 30.5 %all-to-all-start.4 = ((f32[32,1,2000]{2,1,0:T(1,128)}), f32[32,1,2000]{2,1,0:T(1,128)S(1)}, u32[]{:S(2)}, u32[]{:S(2)}) async-start(f32[32,1,2000]{2,1,0:T(1,128)} %reshape.122), calls=%async_computation.4 | async-start | bytes 524288 | tf_op jit(solution)/shard_map/all_to_all | solution.py:111
Sparse Core Ops, SparseCore 0:
  235.5 45.7 all-gather.2
where the time goes:
time: 353 us; the launch traced here: 352 us
  waiting for transfers between devices  224 us (63%)
  starting transfers between devices  62.1 us (18%)
  blocking collectives  16.7 us (5%)
  between operations  14.6 us (4%)
  local copies, waits for them, and re-layouts  14.4 us (4%)
  matrix products  14.3 us (4%)
  other arithmetic  5.68 us (2%)
    all_to_all x2, waiting for transfers between devices, body(): lax.all_to_all(served, 'shard', split_axis=0, concat_axis=0, tiled=True)  99.6 us
    all_to_all x2, waiting for transfers between devices, body(): lax.all_to_all(outgoing, 'shard', split_axis=0, concat_axis=0, tiled=True)  77.6 us
    all_to_all x2, starting transfers between devices, body(): lax.all_to_all(served, 'shard', split_axis=0, concat_axis=0, tiled=True)  26.4 us
    all_to_all x1, waiting for transfers between devices, body(): lax.all_to_all(pieces, 'shard', split_axis=0, concat_axis=0, tiled=True)  21.2 us
    ppermute x4, waiting for transfers between devices, partner(): return lax.ppermute(value, axis, pairs)  20.5 us
    all_to_all x2, starting transfers between devices, body(): lax.all_to_all(outgoing, 'shard', split_axis=0, concat_axis=0, tiled=True)  19 us
    all_gather x1, blocking collectives, body(): ids = lax.all_gather(relation_ids.reshape(-1), 'dom', tiled=True)  16.7 us
    dot_general x29, matrix products, mm(): lax.dot_general(a, b, (((ca,), (cb,)), ((), ())), preferred_element_type=...  14.3 us
  transfers between devices with their start and end apart: 10, of which 10 were waited for; matrix products, arithmetic and copies ran while one was open for 5% of the time, Pallas kernels for 0%

commit v1 on v0

--- a/solution.py
+++ b/solution.py
@@ -102,7 +102,10 @@
         accum = accum + jnp.mean(row_grad * row_grad, axis=-1)
         emb = emb - LEARN_RATE * row_grad / jnp.sqrt(accum)[:, None]
     mine = jnp.concatenate(rel_rows, axis=0)
-    ids = lax.all_gather(relation_ids.reshape(-1), "dom", tiled=True)
+    ids = jnp.concatenate(
+        lax.all_to_all(jnp.stack([relation_ids.reshape(-1)] * lax.axis_size("dom")), "dom", 0, 0),
+        axis=0,
+    )
     group_rows = lax.all_gather(mine, "dom", tiled=True)
     per_group = relations.shape[0] // lax.axis_size("dom")
     local = ids - lax.axis_index("dom").astype(ids.dtype) * per_group

time: 353 us -> 366 us (1.037)
  the two profiles are of different devices: /device:TPU:2 before, /device:TPU:14 now
where the time goes in v1:
time: 366 us; the launch traced here: 365 us
  waiting for transfers between devices  250 us (68%)
  starting transfers between devices  65.4 us (18%)
  local copies, waits for them, and re-layouts  15 us (4%)
  between operations  14.6 us (4%)
  matrix products  14.3 us (4%)
  other arithmetic  5.69 us (2%)
    all_to_all x2, waiting for transfers between devices, body(): lax.all_to_all(served, 'shard', split_axis=0, concat_axis=0, tiled=True)  99.6 us
    all_to_all x2, waiting for transfers between devices, body(): lax.all_to_all(outgoing, 'shard', split_axis=0, concat_axis=0, tiled=True)  91.8 us
    ppermute x4, waiting for transfers between devices, partner(): return lax.ppermute(value, axis, pairs)  29.6 us
    all_to_all x2, starting transfers between devices, body(): lax.all_to_all(served, 'shard', split_axis=0, concat_axis=0, tiled=True)  25.5 us
    all_to_all x1, waiting for transfers between devices, body(): lax.all_to_all(pieces, 'shard', split_axis=0, concat_axis=0, tiled=True)  21.2 us
    all_to_all x2, starting transfers between devices, body(): lax.all_to_all(outgoing, 'shard', split_axis=0, concat_axis=0, tiled=True)  17.4 us
    dot_general x29, matrix products, mm(): lax.dot_general(a, b, (((ca,), (cb,)), ((), ())), preferred_element_type=...  14.3 us
    ppermute x4, starting transfers between devices, partner(): return lax.ppermute(value, axis, pairs)  9.69 us
  transfers between devices with their start and end apart: 11, of which 10 were waited for; matrix products, arithmetic and copies ran while one was open for 5% of the time, Pallas kernels for 0%

profile of v1, /device:TPU:14, one launch (start us, length us, event | category | flops | bytes accessed | tf_op | source)
XLA Modules:
  0.0 364.7 jit_solution(4682791775702241244)
XLA Ops:
  7.2 0.7 fusion.69
  8.1 1.5 convolution_convert_fusion.1
  9.6 1.3 copy.43
  10.9 17.3 %all-to-all-start = ((bf16[32,2,16,400]{3,2,1,0:T(8,128)(2,1)}), bf16[32,2,16,400]{3,2,1,0:T(8,128)(2,1)}, u32[]{:S(2)}, u32[]{:S(2)}) async-start(bf16[32,2,16,400]{3,2,1,0:T(8,128)(2,1)} %bitcast.3), calls=%async_computation | async-start | bytes 2097152 | tf_op jit(solution)/shard_map/all_to_all | solution.py:85
  28.2 2.9 copy.41
  31.2 1.2 gather_fusion
  32.9 47.7 %all-to-all-done = bf16[32,2,16,400]{3,2,1,0:T(8,128)(2,1)} async-done(((bf16[32,2,16,400]{3,2,1,0:T(8,128)(2,1)}), bf16[32,2,16,400]{3,2,1,0:T(8,128)(2,1)}, u32[]{:S(2)}, u32[]{:S(2)}) %all-to-all-start) | async-done | bytes 819232 | tf_op jit(solution)/shard_map/all_to_all | solution.py:85
  80.6 1.3 fusion.68
  81.9 1.9 collective-permute-start
  83.9 1.8 collective-permute-done
  85.7 0.4 fusion.35
  86.1 0.4 fusion.52
  86.5 0.4 fusion.22
  88.9 2.0 collective-permute-start.1
  92.1 0.4 collective-permute-done.1
  92.9 1.1 copy.46
  93.9 7.9 %all-to-all-start.1 = ((bf16[32,2,16,400]{3,2,1,0:T(8,128)(2,1)}), bf16[32,2,16,400]{3,2,1,0:T(8,128)(2,1)S(1)}, u32[]{:S(2)}, u32[]{:S(2)}) async-start(bf16[32,2,16,400]{3,2,1,0:T(8,128)(2,1)} %copy.46), calls=%async_computation.1 | async-start | bytes 2097152 | tf_op jit(solution)/shard_map/all_to_all | solution.py:100
  102.1 52.4 %all-to-all-done.1 = bf16[32,2,16,400]{3,2,1,0:T(8,128)(2,1)S(1)} async-done(((bf16[32,2,16,400]{3,2,1,0:T(8,128)(2,1)}), bf16[32,2,16,400]{3,2,1,0:T(8,128)(2,1)S(1)}, u32[]{:S(2)}, u32[]{:S(2)}) %all-to-all-start.1) | async-done | bytes 819232 | tf_op jit(solution)/shard_map/all_to_all | solution.py:100
  154.4 0.6 multiply_reduce_fusion.3
  155.0 0.6 convolution_convert_fusion
  155.6 1.3 copy.48
  156.9 8.1 %all-to-all-start.2 = ((bf16[32,2,16,400]{3,2,1,0:T(8,128)(2,1)}), bf16[32,2,16,400]{3,2,1,0:T(8,128)(2,1)S(1)}, u32[]{:S(2)}, u32[]{:S(2)}) async-start(bf16[32,2,16,400]{3,2,1,0:T(8,128)(2,1)} %bitcast.13), calls=%async_computation.2 | async-start | bytes 2097152 | tf_op jit(solution)/shard_map/all_to_all | solution.py:85
  165.4 51.9 %all-to-all-done.2 = bf16[32,2,16,400]{3,2,1,0:T(8,128)(2,1)S(1)} async-done(((bf16[32,2,16,400]{3,2,1,0:T(8,128)(2,1)}), bf16[32,2,16,400]{3,2,1,0:T(8,128)(2,1)S(1)}, u32[]{:S(2)}, u32[]{:S(2)}) %all-to-all-start.2) | async-done | bytes 819232 | tf_op jit(solution)/shard_map/all_to_all | solution.py:85
  217.5 3.3 collective-permute-start.2
  220.8 10.8 %collective-permute-done.2 = bf16[512,400]{1,0:T(8,128)(2,1)S(1)} collective-permute-done((bf16[512,400]{1,0:T(8,128)(2,1)S(1)}, bf16[512,400]{1,0:T(8,128)(2,1)S(1)}, u32[]{:S(2)}, u32[]{:S(2)}) %collective-permute-start.2) | collective-permute-done | bytes 409632 | tf_op jit(solution)/shard_map/ppermute | solution.py:14
  231.5 0.4 fusion.29
  231.9 0.4 fusion.53
  232.3 0.4 fusion.24
  233.7 0.7 pad_maximum_fusion.2
  234.5 0.6 stack.14
  235.1 5.7 %all-to-all-start.4 = ((s32[16,1,256]{2,1,0:T(1,128)}), s32[16,1,256]{2,1,0:T(1,128)S(1)}, u32[]{:S(2)}, u32[]{:S(2)}) async-start(s32[16,1,256]{2,1,0:T(1,128)} %stack.14), calls=%async_computation.4 | async-start | bytes 32768 | tf_op jit(solution)/shard_map/all_to_all | solution.py:106
  241.8 2.5 collective-permute-start.3
  245.4 16.6 %collective-permute-done.3 = bf16[512,400]{0,1:T(8,128)(2,1)S(1)} collective-permute-done((bf16[512,400]{0,1:T(8,128)(2,1)S(1)}, bf16[512,400]{0,1:T(8,128)(2,1)S(1)}, u32[]{:S(2)}, u32[]{:S(2)}) %collective-permute-start.3) | collective-permute-done | bytes 409632 | tf_op jit(solution)/shard_map/ppermute | solution.py:14
  262.3 1.1 copy.51
  263.4 9.4 %all-to-all-start.3 = ((bf16[32,2,16,400]{3,2,1,0:T(8,128)(2,1)}), bf16[32,2,16,400]{3,2,1,0:T(8,128)(2,1)S(1)}, u32[]{:S(2)}, u32[]{:S(2)}) async-start(bf16[32,2,16,400]{3,2,1,0:T(8,128)(2,1)} %copy.51), calls=%async_computation.3 | async-start | bytes 2097152 | tf_op jit(solution)/shard_map/all_to_all | solution.py:100
  272.9 7.5 %all-gather.2.cloned.1.call-done = bf16[4096,400]{0,1:T(8,128)(2,1)} async-done(((bf16[256,400]{0,1:T(8,128)(2,1)}), bf16[4096,400]{0,1:T(8,128)(2,1)}) %all-gather.2.cloned.1.call-update) | async-done | bytes 3276816 | tf_op jit(solution)/shard_map/all_gather | solution.py:109
  280.4 3.0 fusion
  283.5 1.3 reshape.130
  284.7 39.4 %all-to-all-done.3 = bf16[32,2,16,400]{3,2,1,0:T(8,128)(2,1)S(1)} async-done(((bf16[32,2,16,400]{3,2,1,0:T(8,128)(2,1)}), bf16[32,2,16,400]{3,2,1,0:T(8,128)(2,1)S(1)}, u32[]{:S(2)}, u32[]{:S(2)}) %all-to-all-start.3) | async-done | bytes 819232 | tf_op jit(solution)/shard_map/all_to_all | solution.py:100
  324.1 7.2 %all-to-all-start.5 = ((f32[32,1,2000]{2,1,0:T(1,128)}), f32[32,1,2000]{2,1,0:T(1,128)S(1)}, u32[]{:S(2)}, u32[]{:S(2)}) async-start(f32[32,1,2000]{2,1,0:T(1,128)} %reshape.130), calls=%async_computation.5 | async-start | bytes 524288 | tf_op jit(solution)/shard_map/all_to_all | solution.py:114
  331.3 0.6 multiply_reduce_fusion.2
  331.9 0.5 fusion.66
  332.4 0.8 divide_subtract_fusion
  333.1 21.2 %all-to-all-done.5 = f32[32,1,2000]{2,1,0:T(1,128)S(1)} async-done(((f32[32,1,2000]{2,1,0:T(1,128)}), f32[32,1,2000]{2,1,0:T(1,128)S(1)}, u32[]{:S(2)}, u32[]{:S(2)}) %all-to-all-start.5) | async-done | bytes 256032 | tf_op jit(solution)/shard_map/all_to_all | solution.py:114
  354.4 0.5 broadcast.120
  354.9 1.3 reduce
  356.6 0.5 fusion.65
  357.2 0.7 multiply_divide_fusion
  (72 shorter events, 9.0 us)
Async XLA Ops:
  10.9 69.8 %all-to-all-start = ((bf16[32,2,16,400]{3,2,1,0:T(8,128)(2,1)}), bf16[32,2,16,400]{3,2,1,0:T(8,128)(2,1)}, u32[]{:S(2)}, u32[]{:S(2)}) async-start(bf16[32,2,16,400]{3,2,1,0:T(8,128)(2,1)} %bitcast.3), calls=%async_computation | async-start | bytes 2097152 | tf_op jit(solution)/shard_map/all_to_all | solution.py:85
  28.2 2.9 copy-start.1
  31.1 1.4 copy-start.2
  31.1 1.6 copy-start.3
  31.1 1.8 copy-start.4
  31.2 52.7 %copy-start.5 = (s32[2,128]{1,0:T(2,128)S(1)}, s32[2,128]{1,0:T(2,128)}, u32[]{:S(2)}) copy-start(s32[2,128]{1,0:T(2,128)} %param.15) | copy-start | bytes 3076
  81.9 3.8 %collective-permute-start = (bf16[512,400]{1,0:T(8,128)(2,1)S(1)}, bf16[512,400]{1,0:T(8,128)(2,1)S(1)}, u32[]{:S(2)}, u32[]{:S(2)}) collective-permute-start(bf16[512,400]{1,0:T(8,128)(2,1)S(1)} %bitcast.73), channel_id=1, source_target_pairs={{0,32},{32,0},{64,96},{96,64},{128,160},{160,128},{192,224},{224,1... | collective-permute-start | bytes 1228808 | tf_op jit(solution)/shard_map/ppermute | solution.py:14
  88.9 3.6 collective-permute-start.1
  92.8 62.1 %copy-start.6 = (f32[64]{0:T(128)S(1)}, f32[64]{0:T(128)}, u32[]{:S(2)}) copy-start(f32[64]{0:T(128)} %param.11) | copy-start | bytes 772
  92.9 62.2 %copy-start = (f32[64,400]{1,0:T(8,128)S(1)}, f32[64,400]{1,0:T(8,128)}, u32[]{:S(2)}) copy-start(f32[64,400]{1,0:T(8,128)} %param.10) | copy-start | bytes 307204
  93.9 60.5 %all-to-all-start.1 = ((bf16[32,2,16,400]{3,2,1,0:T(8,128)(2,1)}), bf16[32,2,16,400]{3,2,1,0:T(8,128)(2,1)S(1)}, u32[]{:S(2)}, u32[]{:S(2)}) async-start(bf16[32,2,16,400]{3,2,1,0:T(8,128)(2,1)} %copy.46), calls=%async_computation.1 | async-start | bytes 2097152 | tf_op jit(solution)/shard_map/all_to_all | solution.py:100
  156.9 60.5 %all-to-all-start.2 = ((bf16[32,2,16,400]{3,2,1,0:T(8,128)(2,1)}), bf16[32,2,16,400]{3,2,1,0:T(8,128)(2,1)S(1)}, u32[]{:S(2)}, u32[]{:S(2)}) async-start(bf16[32,2,16,400]{3,2,1,0:T(8,128)(2,1)} %bitcast.13), calls=%async_computation.2 | async-start | bytes 2097152 | tf_op jit(solution)/shard_map/all_to_all | solution.py:85
  165.0 115.3 %all-gather.2.cloned.1.call-start = ((), (), s32[]{:S(2)}) async-start(), calls=%async_computation.6 | async-start | bytes 3481600 | tf_op jit(solution)/shard_map/all_gather | solution.py:109
  217.5 14.1 %collective-permute-start.2 = (bf16[512,400]{1,0:T(8,128)(2,1)S(1)}, bf16[512,400]{1,0:T(8,128)(2,1)S(1)}, u32[]{:S(2)}, u32[]{:S(2)}) collective-permute-start(bf16[512,400]{1,0:T(8,128)(2,1)S(1)} %bitcast.74), channel_id=1, source_target_pairs={{0,64},{32,96},{64,0},{96,32},{128,192},{160,224},{192,128},{224,1... | collective-permute-start | bytes 1228808 | tf_op jit(solution)/shard_map/ppermute | solution.py:14
  235.1 28.3 %all-to-all-start.4 = ((s32[16,1,256]{2,1,0:T(1,128)}), s32[16,1,256]{2,1,0:T(1,128)S(1)}, u32[]{:S(2)}, u32[]{:S(2)}) async-start(s32[16,1,256]{2,1,0:T(1,128)} %stack.14), calls=%async_computation.4 | async-start | bytes 32768 | tf_op jit(solution)/shard_map/all_to_all | solution.py:106
  241.8 20.2 %collective-permute-start.3 = (bf16[512,400]{0,1:T(8,128)(2,1)S(1)}, bf16[512,400]{0,1:T(8,128)(2,1)S(1)}, u32[]{:S(2)}, u32[]{:S(2)}) collective-permute-start(bf16[512,400]{0,1:T(8,128)(2,1)S(1)} %fusion.5), channel_id=1, source_target_pairs={{0,64},{32,96},{64,0},{96,32},{128,192},{160,224},{192,128},{224,1... | collective-permute-start | bytes 1228808 | tf_op jit(solution)/shard_map/ppermute | solution.py:14
  263.4 60.7 %all-to-all-start.3 = ((bf16[32,2,16,400]{3,2,1,0:T(8,128)(2,1)}), bf16[32,2,16,400]{3,2,1,0:T(8,128)(2,1)S(1)}, u32[]{:S(2)}, u32[]{:S(2)}) async-start(bf16[32,2,16,400]{3,2,1,0:T(8,128)(2,1)} %copy.51), calls=%async_computation.3 | async-start | bytes 2097152 | tf_op jit(solution)/shard_map/all_to_all | solution.py:100
  283.5 73.2 %copy-start.7 = (f32[5]{0:T(128)S(1)}, f32[5]{0:T(128)}, u32[]{:S(2)}) copy-start(f32[5]{0:T(128)} %param.13) | copy-start | bytes 64
  324.1 30.2 %all-to-all-start.5 = ((f32[32,1,2000]{2,1,0:T(1,128)}), f32[32,1,2000]{2,1,0:T(1,128)S(1)}, u32[]{:S(2)}, u32[]{:S(2)}) async-start(f32[32,1,2000]{2,1,0:T(1,128)} %reshape.130), calls=%async_computation.5 | async-start | bytes 524288 | tf_op jit(solution)/shard_map/all_to_all | solution.py:114
Sparse Core Ops, SparseCore 0:
  234.6 45.7 all-gather.1
